TPU v7x, 32 devices: a whole 2x2x4 slice. The times are simulated.
32 devices in a mesh: regroup: 2 (over y), loop: 4 (over z), replica: 4 (over x, core).
Axes of the slice: x: 2, y: 2, z: 4, core: 2. Of those that a mesh axis runs over, the one named last changes fastest.
Arguments:
- features: bfloat16 [4, 4, 1024, 256], P('replica', 'loop', None, 'regroup'), may hold values from -6 to 6
- weight: bfloat16 [256, 256], replicated, may hold values from -0.375 to 0.375
- tiles: bfloat16 [4, 4, 2, 32, 128, 128], P('replica', 'loop', 'regroup'), may hold values from 0 to 1, as said below
- tile_row: int32 [4, 4, 2, 32], P('replica', 'loop', 'regroup'), may hold values from 0 to 3, as said below
- tile_col: int32 [4, 4, 2, 32], P('replica', 'loop', 'regroup'), may hold values from 0 to 3, as said below
- tile_width: int32 [4, 4, 2, 32], P('replica', 'loop', 'regroup'), may hold values from 0 to 128, as said below
- cotangent: bfloat16 [4, 4, 2, 512, 256], P('replica', 'loop', 'regroup'), may hold values from -6 to 6
Outputs:
- output: bfloat16 [4, 4, 2, 512, 256], P('replica', 'loop', 'regroup')
- grad_feat: bfloat16 [4, 4, 1024, 256], P('replica', 'loop', None, 'regroup')
- grad_weight: float32 [256, 256], replicated
Inputs may be any that keep to these rules, and one draw needn't show every extreme that they name: `tiles`: entries are 0 or between 0.25 and 1. `tile_row`: slot k < 4 of every device names cell block k. tile_col[r, l, g, s] is l - 1, l or l + 1 modulo 4. `tile_width`: each device's live slots come first, from 4 to 32 of them; some device has exactly 4 live and some all 32; slot 0 is live with width 128.
All inputs are finite; a program needn't handle non-finite values.
Results may differ from a plain program's by a relative error of at most 0.013.
Values may be sent and summed in bfloat16 or wider, within the bound.
A program may use at most 64 MiB of HBM per device.

v0:
```python
import math
import jax
import jax.numpy as jnp
from jax import lax
from jax.sharding import PartitionSpec as P

EPSILON = 1e-06


def shifted(block, axis, distance):
    devices = range(lax.axis_size(axis))
    route = [((i - distance) % len(devices), i) for i in devices]
    return lax.ppermute(block, axis, route)


def rms_scale(values):
    return values * lax.rsqrt(jnp.mean(values * values, axis=-1, keepdims=True) + EPSILON)


def per_device(features, weight, tiles, tile_row, tile_col, tile_width, cotangent):
    cell_rows = lax.all_to_all(features, "regroup", split_axis=2, concat_axis=3, tiled=True)[0, 0]
    cells, width = cell_rows.shape
    edge = tiles.shape[-1]
    blocks = cells // edge
    loops = lax.axis_size("loop")
    high = lax.Precision.HIGHEST
    rows_idx = tile_row[0, 0, 0]
    cols_idx = tile_col[0, 0, 0]
    widths = tile_width[0, 0, 0]
    column = jnp.arange(edge, dtype=jnp.int32)
    live_tiles = jnp.where(
        column[None, None, :] < widths[:, None, None], tiles[0, 0, 0], jnp.zeros((), tiles.dtype)
    )
    row_hot = (rows_idx[:, None] == jnp.arange(blocks, dtype=jnp.int32)[None, :]).astype(
        jnp.float32
    )
    row_sums = jnp.sum(live_tiles, axis=2, dtype=jnp.float32)
    cell_deg = 1.0 + jnp.einsum("tr,ti->ri", row_hot, row_sums, precision=high).reshape(cells)
    cell_root = jnp.sqrt(cell_deg)[:, None]
    col_tile_sums = jnp.sum(live_tiles, axis=1, dtype=jnp.float32)

    def to_nets(values, hot):
        gathered = values.reshape(blocks, edge, width)[rows_idx]
        per_tile = jnp.einsum(
            "tij,tif->tjf", live_tiles, gathered, preferred_element_type=jnp.float32
        )
        return jnp.einsum("tc,tjf->cjf", hot, per_tile, precision=high)

    def from_nets(blocked, index):
        gathered = blocked[index]
        per_tile = jnp.einsum(
            "tij,tjf->tif", live_tiles, gathered, preferred_element_type=jnp.float32
        )
        return jnp.einsum("tr,tif->rif", row_hot, per_tile, precision=high).reshape(cells, width)

    mixed = jnp.dot(cell_rows, weight, preferred_element_type=jnp.float32).astype(jnp.bfloat16)
    scaled = (mixed.astype(jnp.float32) / cell_root).astype(jnp.bfloat16)
    place = (cols_idx - lax.axis_index("loop") + loops) % loops
    net_index = jnp.where(place == 0, 1, jnp.where(place == 1, 2, 0)).astype(jnp.int32)
    near_hot = (net_index[:, None] == jnp.arange(3, dtype=jnp.int32)[None, :]).astype(jnp.float32)
    near_terms = to_nets(scaled, near_hot).astype(jnp.bfloat16)
    near_degs = jnp.einsum("tc,tj->cj", near_hot, col_tile_sums, precision=high).astype(
        jnp.bfloat16
    )
    below = shifted((near_terms[2], near_degs[2]), "loop", 1)
    above = shifted((near_terms[0], near_degs[0]), "loop", -1)
    totals = (
        near_terms[1].astype(jnp.float32)
        + below[0].astype(jnp.float32)
        + above[0].astype(jnp.float32)
    )
    degrees = (
        near_degs[1].astype(jnp.float32)
        + below[1].astype(jnp.float32)
        + above[1].astype(jnp.float32)
    )
    net_deg = (1.0 + degrees)[:, None]
    own_feat = (totals / net_deg).astype(jnp.bfloat16)
    prev_feat = shifted(own_feat, "loop", 1)
    next_feat = shifted(own_feat, "loop", -1)
    net_feat = jnp.stack([prev_feat, own_feat, next_feat])
    gathered_z = from_nets(net_feat, net_index) / cell_root
    normed, norm_back = jax.vjp(rms_scale, gathered_z)
    before = mixed.astype(jnp.float32) + normed
    output = jax.nn.silu(before).astype(jnp.bfloat16)
    sigmoid_v = jax.nn.sigmoid(before)
    grad_before = (
        cotangent[0, 0, 0].astype(jnp.float32) * sigmoid_v * (1.0 + before * (1.0 - sigmoid_v))
    )
    grad_z = norm_back(grad_before)[0]
    grad_scaled = (grad_z / cell_root).astype(jnp.bfloat16)
    grad_near = to_nets(grad_scaled, near_hot).astype(jnp.bfloat16)
    grad_below = shifted(grad_near[2], "loop", 1)
    grad_above = shifted(grad_near[0], "loop", -1)
    grad_sum_own = (
        grad_near[1].astype(jnp.float32)
        + grad_below.astype(jnp.float32)
        + grad_above.astype(jnp.float32)
    )
    grad_own = (grad_sum_own / net_deg).astype(jnp.bfloat16)
    grad_prev = shifted(grad_own, "loop", 1)
    grad_next = shifted(grad_own, "loop", -1)
    grad_net = jnp.stack([grad_prev, grad_own, grad_next])
    grad_mixed = (grad_before + from_nets(grad_net, net_index) / cell_root).astype(jnp.bfloat16)
    grad_rows = jnp.einsum(
        "cg,fg->cf", grad_mixed, weight, preferred_element_type=jnp.float32
    ).astype(jnp.bfloat16)
    grad_feat = lax.all_to_all(
        grad_rows[None, None], "regroup", split_axis=3, concat_axis=2, tiled=True
    )
    weight_term = jnp.einsum("cf,cg->fg", cell_rows, grad_mixed, preferred_element_type=jnp.float32)
    weight_part = lax.psum_scatter(
        weight_term, ("regroup", "loop"), scatter_dimension=0, tiled=True
    )
    weight_part = lax.psum(weight_part, "replica")
    weight_sum = lax.all_gather(weight_part, ("regroup", "loop"), axis=0, tiled=True)
    total_cells = cells * lax.axis_size("regroup") * loops * lax.axis_size("replica")
    grad_weight = weight_sum * (1.0 / math.sqrt(total_cells))
    return (output[None, None, None], grad_feat, grad_weight)


def solution(mesh):
    return jax.shard_map(
        per_device,
        mesh=mesh,
        in_specs=(
            P("replica", "loop", None, "regroup"),
            P(),
            P("replica", "loop", "regroup", None, None, None),
            P("replica", "loop", "regroup", None),
            P("replica", "loop", "regroup", None),
            P("replica", "loop", "regroup", None),
            P("replica", "loop", "regroup", None, None),
        ),
        out_specs=(
            P("replica", "loop", "regroup", None, None),
            P("replica", "loop", None, "regroup"),
            P(),
        ),
        check_vma=False,
    )
```

profile of v0, /device:TPU:0, one launch (start us, length us, event | category | flops | bytes accessed | tf_op | source)
XLA Modules:
  0.0 198.6 jit_solution(6420533877653232573)
XLA Ops:
  7.2 0.8 iota_compare_fusion
  8.0 0.7 compare_select_fusion.8
  8.6 1.6 convert_reduce_fusion
  10.4 0.6 slice_bitcast_fusion.4
  11.0 3.0 %collective-permute-start.2 = (bf16[128]{0:T(256)(128)(2,1)}, bf16[128]{0:T(256)(128)(2,1)}, u32[]{:S(2)}, u32[]{:S(2)}) collective-permute-start(bf16[128]{0:T(256)(128)(2,1)} %get-tuple-element.22), channel_id=1, source_target_pairs={{12,0},{0,4},{4,8},{8,12},{13,1},{1,5},{5,9},{9,13},{14,2},{2,6},{... | collective-permute-start | bytes 776 | tf_op jit(solution)/shard_map/ppermute | solution.py:13
  14.0 2.0 %collective-permute-start.3 = (bf16[128]{0:T(256)(128)(2,1)}, bf16[128]{0:T(256)(128)(2,1)}, u32[]{:S(2)}, u32[]{:S(2)}) collective-permute-start(bf16[128]{0:T(256)(128)(2,1)} %get-tuple-element.23), channel_id=1, source_target_pairs={{4,0},{8,4},{12,8},{0,12},{5,1},{9,5},{13,9},{1,13},{6,2},{10,6},{... | collective-permute-start | bytes 776 | tf_op jit(solution)/shard_map/ppermute | solution.py:13
  16.0 1.4 copy.130
  17.4 0.5 broadcast.232
  17.9 2.3 %reduce.1 = bf16[1024,128]{1,0:T(8,128)(2,1)S(1)} reduce(bf16[1024,1,1,128]{3,2,1,0:T(2,128)(2,1)S(1)} %bitcast.136, bf16[]{:T(256)} %broadcast.232), dimensions={1,2}, to_apply=%bitcast.131.reduce_sub_computation | reduce | bytes 524290
  20.2 0.8 reshape.232
  20.9 3.4 %all-to-all-start = ((bf16[2,2,32768]{2,1,0:T(2,128)(2,1)}), bf16[2,2,32768]{2,1,0:T(2,128)(2,1)S(1)}, u32[]{:S(2)}, u32[]{:S(2)}) async-start(bf16[2,2,32768]{2,1,0:T(2,128)(2,1)} %reshape.232), calls=%async_computation | async-start | bytes 524288 | tf_op jit(solution)/shard_map/all_to_all | solution.py:21
  24.4 0.6 fusion.43
  25.0 0.1 fusion.13
  25.2 0.8 copy.90
  25.9 3.6 %all-to-all-done = bf16[2,2,32768]{2,1,0:T(2,128)(2,1)S(1)} async-done(((bf16[2,2,32768]{2,1,0:T(2,128)(2,1)}), bf16[2,2,32768]{2,1,0:T(2,128)(2,1)S(1)}, u32[]{:S(2)}, u32[]{:S(2)}) %all-to-all-start) | async-done | bytes 262176 | tf_op jit(solution)/shard_map/all_to_all | solution.py:21
  29.5 0.3 reshape.233
  29.9 0.1 copy.85
  30.0 1.1 divide_convert_fusion
  31.1 0.7 gather_fusion
  31.8 0.5 copy-done.1
  32.3 0.8 fusion.23
  33.1 3.8 %fusion.9 = bf16[3,128,256]{2,0,1:T(4,128)(2,1)S(1)} fusion(f32[32,128,256]{2,1,0:T(8,128)S(1)} %fusion.23, s32[32]{0:T(128)S(1)} %copy-done.10), kind=kOutput, calls=%fused_computation.17 | convolution fusion | flops 37847136 | bytes 4391040 | tf_op jit(solution)/shard_map/tc,tjf->cjf/dot_general | solution.py:47
  37.0 0.3 fusion.54
  37.3 2.1 %collective-permute-start.1 = (bf16[128,256]{1,0:T(8,128)(2,1)S(1)}, bf16[128,256]{1,0:T(8,128)(2,1)S(1)}, u32[]{:S(2)}, u32[]{:S(2)}) collective-permute-start(bf16[128,256]{1,0:T(8,128)(2,1)S(1)} %bitcast.146), channel_id=1, source_target_pairs={{4,0},{8,4},{12,8},{0,12},{5,1},{9,5},{13,9},{1,13},{6,2},{10,6},{... | collective-permute-start | bytes 196616 | tf_op jit(solution)/shard_map/ppermute | solution.py:13
  39.4 0.7 fusion.48
  40.0 1.6 collective-permute-done.1
  41.6 3.8 %collective-permute-done = bf16[128,256]{1,0:T(8,128)(2,1)S(1)} collective-permute-done((bf16[128,256]{1,0:T(8,128)(2,1)S(1)}, bf16[128,256]{1,0:T(8,128)(2,1)S(1)}, u32[]{:S(2)}, u32[]{:S(2)}) %collective-permute-start) | collective-permute-done | bytes 65568 | tf_op jit(solution)/shard_map/ppermute | solution.py:13
  45.6 2.0 %collective-permute-start.4 = (bf16[128,256]{1,0:T(8,128)(2,1)S(1)}, bf16[128,256]{1,0:T(8,128)(2,1)S(1)}, u32[]{:S(2)}, u32[]{:S(2)}) collective-permute-start(bf16[128,256]{1,0:T(8,128)(2,1)S(1)} %fusion.27), channel_id=1, source_target_pairs={{12,0},{0,4},{4,8},{8,12},{13,1},{1,5},{5,9},{9,13},{14,2},{2,6},{... | collective-permute-start | bytes 196616 | tf_op jit(solution)/shard_map/ppermute | solution.py:13
  47.6 2.2 %collective-permute-done.5 = bf16[128,256]{1,0:T(8,128)(2,1)S(1)} collective-permute-done((bf16[128,256]{1,0:T(8,128)(2,1)S(1)}, bf16[128,256]{1,0:T(8,128)(2,1)S(1)}, u32[]{:S(2)}, u32[]{:S(2)}) %collective-permute-start.5) | collective-permute-done | bytes 65568 | tf_op jit(solution)/shard_map/ppermute | solution.py:13
  49.8 2.0 %collective-permute-done.4 = bf16[128,256]{1,0:T(8,128)(2,1)S(1)} collective-permute-done((bf16[128,256]{1,0:T(8,128)(2,1)S(1)}, bf16[128,256]{1,0:T(8,128)(2,1)S(1)}, u32[]{:S(2)}, u32[]{:S(2)}) %collective-permute-start.4) | collective-permute-done | bytes 65568 | tf_op jit(solution)/shard_map/ppermute | solution.py:13
  51.9 0.7 gather_fusion.1
  52.6 0.7 fusion.22
  53.5 4.0 %fusion.19 = (f32[4,128]{0,1:T(8,128)S(1)}, f32[4,128,256]{2,0,1:T(4,128)S(1)}) fusion(f32[4,128]{0,1:T(8,128)S(1)} %copy-done.8, f32[32,128,256]{2,1,0:T(8,128)S(1)} %fusion.22, s32[32]{0:T(128)S(1)} %bitcast.156), kind=kOutput, calls=%fused_computation.39 | convolution fusion | flops 50724480 | bytes 4722816 | tf_op jit(solution)/shard_map/tr,tif->rif/dot_general | solution.py:54
  57.6 0.1 copy.89
  57.7 1.1 multiply_reduce_fusion
  58.8 0.3 fusion.15
  59.1 0.5 copy-done.2
  59.6 0.7 gather_fusion.2
  60.3 0.8 fusion.21
  61.1 3.8 %fusion.2 = bf16[3,128,256]{2,0,1:T(4,128)(2,1)S(1)} fusion(f32[32,128,256]{2,1,0:T(8,128)S(1)} %fusion.21, s32[32]{0:T(128)S(1)} %copy-done.11), kind=kOutput, calls=%fused_computation.6 | convolution fusion | flops 37748832 | bytes 4391040 | tf_op jit(solution)/shard_map/tc,tjf->cjf/dot_general | solution.py:47
  65.0 3.8 %collective-permute-start.7 = (bf16[128,256]{1,0:T(8,128)(2,1)S(1)}, bf16[128,256]{1,0:T(8,128)(2,1)S(1)}, u32[]{:S(2)}, u32[]{:S(2)}) collective-permute-start(bf16[128,256]{1,0:T(8,128)(2,1)S(1)} %get-tuple-element.21), channel_id=1, source_target_pairs={{4,0},{8,4},{12,8},{0,12},{5,1},{9,5},{13,9},{1,13},{6,2},{10,6},{... | collective-permute-start | bytes 196616 | tf_op jit(solution)/shard_map/ppermute | solution.py:13
  68.9 2.2 %collective-permute-done.6 = bf16[128,256]{1,0:T(8,128)(2,1)S(1)} collective-permute-done((bf16[128,256]{1,0:T(8,128)(2,1)S(1)}, bf16[128,256]{1,0:T(8,128)(2,1)S(1)}, u32[]{:S(2)}, u32[]{:S(2)}) %collective-permute-start.6) | collective-permute-done | bytes 65568 | tf_op jit(solution)/shard_map/ppermute | solution.py:13
  71.2 4.2 %collective-permute-start.9 = (bf16[128,256]{1,0:T(8,128)(2,1)S(1)}, bf16[128,256]{1,0:T(8,128)(2,1)S(1)}, u32[]{:S(2)}, u32[]{:S(2)}) collective-permute-start(bf16[128,256]{1,0:T(8,128)(2,1)S(1)} %fusion.30), channel_id=1, source_target_pairs={{4,0},{8,4},{12,8},{0,12},{5,1},{9,5},{13,9},{1,13},{6,2},{10,6},{... | collective-permute-start | bytes 196616 | tf_op jit(solution)/shard_map/ppermute | solution.py:13
  75.4 1.9 collective-permute-done.9
  77.3 4.2 %collective-permute-done.8 = bf16[128,256]{1,0:T(8,128)(2,1)S(1)} collective-permute-done((bf16[128,256]{1,0:T(8,128)(2,1)S(1)}, bf16[128,256]{1,0:T(8,128)(2,1)S(1)}, u32[]{:S(2)}, u32[]{:S(2)}) %collective-permute-start.8) | collective-permute-done | bytes 65568 | tf_op jit(solution)/shard_map/ppermute | solution.py:13
  81.5 0.7 gather_fusion.3
  82.2 0.7 fusion.20
  82.9 3.8 %fusion = f32[4,128,256]{2,0,1:T(4,128)S(1)} fusion(f32[32,128,256]{2,1,0:T(8,128)S(1)} %fusion.20, s32[32]{0:T(128)S(1)} %bitcast.157), kind=kOutput, calls=%fused_computation.4 | convolution fusion | flops 50331776 | bytes 4718720 | tf_op jit(solution)/shard_map/tr,tif->rif/dot_general | solution.py:54
  86.8 0.1 fusion.18
  87.0 0.7 copy-done.5
  87.6 0.3 convolution_bitcast_fusion
  87.9 0.8 copy.102
  88.8 0.3 fusion.12
  89.0 0.5 copy.97
  89.5 2.2 %reduce.2 = bf16[256,512]{1,0:T(8,128)(2,1)S(1)} reduce(bf16[256,1,1,512]{3,2,1,0:T(2,128)(2,1)S(1)} %bitcast.137, bf16[]{:T(256)} %broadcast.232), dimensions={1,2}, to_apply=%bitcast.110.reduce_sub_computation | reduce | bytes 524290
  91.7 0.2 reshape.234
  91.9 7.6 %all_to_all.33 = bf16[2,2,32768]{2,1,0:T(2,128)(2,1)S(1)} all-to-all(bf16[2,2,32768]{2,1,0:T(2,128)(2,1)S(1)} %reshape.234), channel_id=1, replica_groups=mesh['regroup'=2,'loop'=4,'replica'=4] {'regroup'}, dimensions={0} | all-to-all | bytes 524288 | tf_op jit(solution)/shard_map/all_to_all | solution.py:108
  99.5 0.3 reshape.235
  99.8 0.8 copy.98
  100.6 46.8 %reduce-scatter.4.cloned.1.call-done = f32[32,256]{1,0:T(8,128)} async-done(((f32[256,256]{1,0:T(8,128)}), f32[32,256]{1,0:T(8,128)}) %reduce-scatter.4.cloned.1.call-update) | async-done | bytes 32784
  147.4 0.9 copy.103
  148.2 11.5 %psum.7 = f32[32,256]{0,1:T(8,128)S(1)} all-reduce(f32[32,256]{0,1:T(8,128)S(1)} %copy.103), channel_id=1, replica_groups=mesh['regroup'=2,'loop'=4,'replica'=4] {'replica'}, use_global_device_ids=true, to_apply=%region_5.6 | all-reduce | flops 8192 | bytes 65536 | tf_op jit(solution)/shard_map/psum | solution.py:115
  159.8 31.3 %all_gather.3 = f32[256,256]{1,0:T(8,128)S(1)} all-gather(f32[32,256]{1,0:T(8,128)S(1)} %copy.99), channel_id=1, replica_groups=mesh['regroup'=2,'loop'=4,'replica'=4] {'regroup','loop'}, dimensions={0}, use_global_device_ids=true | all-gather | bytes 294912 | tf_op jit(solution)/shard_map/all_gather | solution.py:116
  191.1 0.7 broadcast_multiply_fusion
  (64 shorter events, 1.1 us)
Async XLA Ops:
  7.2 22.9 %copy-start = (bf16[256,256]{1,0:T(8,128)(2,1)S(1)}, bf16[256,256]{1,0:T(8,128)(2,1)}, u32[]{:S(2)}) copy-start(bf16[256,256]{1,0:T(8,128)(2,1)} %param.8) | copy-start | bytes 393220
  7.2 17.3 %copy-start.18 = (s32[1,1,1,32]{3,2,1,0:T(1,128)S(1)}, s32[1,1,1,32]{3,2,1,0:T(1,128)}, u32[]{:S(2)}) copy-start(s32[1,1,1,32]{3,2,1,0:T(1,128)} %param.11) | copy-start | bytes 388
  7.2 17.8 %copy-start.14 = (s32[1,1,1,32]{3,2,1,0:T(1,128)S(1)}, s32[1,1,1,32]{3,2,1,0:T(1,128)}, u32[]{:S(2)}) copy-start(s32[1,1,1,32]{3,2,1,0:T(1,128)} %param.10) | copy-start | bytes 388
  8.6 16.4 %copy-start.9 = (s32[32]{0:T(128)}, s32[32]{0:T(128)S(1)}, u32[]{:S(2)}) copy-start(s32[32]{0:T(128)S(1)} %compare_select_fusion.8) | copy-start | bytes 388
  11.0 28.4 %collective-permute-start.2 = (bf16[128]{0:T(256)(128)(2,1)}, bf16[128]{0:T(256)(128)(2,1)}, u32[]{:S(2)}, u32[]{:S(2)}) collective-permute-start(bf16[128]{0:T(256)(128)(2,1)} %get-tuple-element.22), channel_id=1, source_target_pairs={{12,0},{0,4},{4,8},{8,12},{13,1},{1,5},{5,9},{9,13},{14,2},{2,6},{... | collective-permute-start | bytes 776 | tf_op jit(solution)/shard_map/ppermute | solution.py:13
  14.0 25.4 %collective-permute-start.3 = (bf16[128]{0:T(256)(128)(2,1)}, bf16[128]{0:T(256)(128)(2,1)}, u32[]{:S(2)}, u32[]{:S(2)}) collective-permute-start(bf16[128]{0:T(256)(128)(2,1)} %get-tuple-element.23), channel_id=1, source_target_pairs={{4,0},{8,4},{12,8},{0,12},{5,1},{9,5},{13,9},{1,13},{6,2},{10,6},{... | collective-permute-start | bytes 776 | tf_op jit(solution)/shard_map/ppermute | solution.py:13
  20.9 8.6 %all-to-all-start = ((bf16[2,2,32768]{2,1,0:T(2,128)(2,1)}), bf16[2,2,32768]{2,1,0:T(2,128)(2,1)S(1)}, u32[]{:S(2)}, u32[]{:S(2)}) async-start(bf16[2,2,32768]{2,1,0:T(2,128)(2,1)} %reshape.232), calls=%async_computation | async-start | bytes 524288 | tf_op jit(solution)/shard_map/all_to_all | solution.py:21
  24.4 123.0 %reduce-scatter.4.cloned.1.call-start = ((), (), s32[]{:S(2)}) async-start(), calls=%async_computation.3 | async-start | bytes 294912
  30.0 1.1 copy-start.4
  31.1 1.2 copy-start.1
  32.3 0.8 copy-start.10
  33.1 14.5 %copy-start.17 = (s32[32]{0:T(128)S(1)}, s32[32]{0:T(128)}, u32[]{:S(2)}) copy-start(s32[32]{0:T(128)} %fusion.43) | copy-start | bytes 388
  37.3 4.3 %collective-permute-start.1 = (bf16[128,256]{1,0:T(8,128)(2,1)S(1)}, bf16[128,256]{1,0:T(8,128)(2,1)S(1)}, u32[]{:S(2)}, u32[]{:S(2)}) collective-permute-start(bf16[128,256]{1,0:T(8,128)(2,1)S(1)} %bitcast.146), channel_id=1, source_target_pairs={{4,0},{8,4},{12,8},{0,12},{5,1},{9,5},{13,9},{1,13},{6,2},{10,6},{... | collective-permute-start | bytes 196616 | tf_op jit(solution)/shard_map/ppermute | solution.py:13
  39.4 6.1 %collective-permute-start = (bf16[128,256]{1,0:T(8,128)(2,1)S(1)}, bf16[128,256]{1,0:T(8,128)(2,1)S(1)}, u32[]{:S(2)}, u32[]{:S(2)}) collective-permute-start(bf16[128,256]{1,0:T(8,128)(2,1)S(1)} %bitcast.145), channel_id=1, source_target_pairs={{12,0},{0,4},{4,8},{8,12},{13,1},{1,5},{5,9},{9,13},{14,2},{2,6},{... | collective-permute-start | bytes 196616 | tf_op jit(solution)/shard_map/ppermute | solution.py:13
  40.0 11.9 %copy-start.12 = (f32[128]{0:T(128)}, f32[128]{0:T(128)S(1)}, u32[]{:S(2)}) copy-start(f32[128]{0:T(128)S(1)} %fusion.48) | copy-start | bytes 1540
  45.5 4.3 %collective-permute-start.5 = (bf16[128,256]{1,0:T(8,128)(2,1)S(1)}, bf16[128,256]{1,0:T(8,128)(2,1)S(1)}, u32[]{:S(2)}, u32[]{:S(2)}) collective-permute-start(bf16[128,256]{1,0:T(8,128)(2,1)S(1)} %fusion.27), channel_id=1, source_target_pairs={{4,0},{8,4},{12,8},{0,12},{5,1},{9,5},{13,9},{1,13},{6,2},{10,6},{... | collective-permute-start | bytes 196616 | tf_op jit(solution)/shard_map/ppermute | solution.py:13
  45.6 6.3 %collective-permute-start.4 = (bf16[128,256]{1,0:T(8,128)(2,1)S(1)}, bf16[128,256]{1,0:T(8,128)(2,1)S(1)}, u32[]{:S(2)}, u32[]{:S(2)}) collective-permute-start(bf16[128,256]{1,0:T(8,128)(2,1)S(1)} %fusion.27), channel_id=1, source_target_pairs={{12,0},{0,4},{4,8},{8,12},{13,1},{1,5},{5,9},{9,13},{14,2},{2,6},{... | collective-permute-start | bytes 196616 | tf_op jit(solution)/shard_map/ppermute | solution.py:13
  52.6 0.8 copy-start.8
  52.6 0.8 copy-start.15
  53.4 4.2 %copy-start.6 = (f32[512,256]{1,0:T(8,128)S(1)}, f32[512,256]{1,0:T(8,128)}, u32[]{:S(2)}) copy-start(f32[512,256]{1,0:T(8,128)} %get-tuple-element.25) | copy-start | bytes 1572868
  53.5 4.2 %copy-start.7 = (bf16[1,1,1,512,256]{4,3,2,1,0:T(8,128)(2,1)S(1)}, bf16[1,1,1,512,256]{4,3,2,1,0:T(8,128)(2,1)}, u32[]{:S(2)}) copy-start(bf16[1,1,1,512,256]{4,3,2,1,0:T(8,128)(2,1)} %param.13) | copy-start | bytes 786436
  58.8 0.8 copy-start.2
  60.3 0.8 copy-start.11
  61.1 10.0 %copy-start.13 = (f32[128]{0:T(128)S(1)}, f32[128]{0:T(128)}, u32[]{:S(2)}) copy-start(f32[128]{0:T(128)} %copy-done.12) | copy-start | bytes 1540
  65.0 6.1 %collective-permute-start.6 = (bf16[128,256]{1,0:T(8,128)(2,1)S(1)}, bf16[128,256]{1,0:T(8,128)(2,1)S(1)}, u32[]{:S(2)}, u32[]{:S(2)}) collective-permute-start(bf16[128,256]{1,0:T(8,128)(2,1)S(1)} %get-tuple-element.20), channel_id=1, source_target_pairs={{12,0},{0,4},{4,8},{8,12},{13,1},{1,5},{5,9},{9,13},{14,2},{2,6},{... | collective-permute-start | bytes 196616 | tf_op jit(solution)/shard_map/ppermute | solution.py:13
  65.0 6.1 %collective-permute-start.7 = (bf16[128,256]{1,0:T(8,128)(2,1)S(1)}, bf16[128,256]{1,0:T(8,128)(2,1)S(1)}, u32[]{:S(2)}, u32[]{:S(2)}) collective-permute-start(bf16[128,256]{1,0:T(8,128)(2,1)S(1)} %get-tuple-element.21), channel_id=1, source_target_pairs={{4,0},{8,4},{12,8},{0,12},{5,1},{9,5},{13,9},{1,13},{6,2},{10,6},{... | collective-permute-start | bytes 196616 | tf_op jit(solution)/shard_map/ppermute | solution.py:13
  71.2 6.1 %collective-permute-start.9 = (bf16[128,256]{1,0:T(8,128)(2,1)S(1)}, bf16[128,256]{1,0:T(8,128)(2,1)S(1)}, u32[]{:S(2)}, u32[]{:S(2)}) collective-permute-start(bf16[128,256]{1,0:T(8,128)(2,1)S(1)} %fusion.30), channel_id=1, source_target_pairs={{4,0},{8,4},{12,8},{0,12},{5,1},{9,5},{13,9},{1,13},{6,2},{10,6},{... | collective-permute-start | bytes 196616 | tf_op jit(solution)/shard_map/ppermute | solution.py:13
  75.4 6.1 %collective-permute-start.8 = (bf16[128,256]{1,0:T(8,128)(2,1)S(1)}, bf16[128,256]{1,0:T(8,128)(2,1)S(1)}, u32[]{:S(2)}, u32[]{:S(2)}) collective-permute-start(bf16[128,256]{1,0:T(8,128)(2,1)S(1)} %fusion.30), channel_id=1, source_target_pairs={{12,0},{0,4},{4,8},{8,12},{13,1},{1,5},{5,9},{9,13},{14,2},{2,6},{... | collective-permute-start | bytes 196616 | tf_op jit(solution)/shard_map/ppermute | solution.py:13
  82.1 0.7 copy-start.16
  82.9 3.9 %copy-start.3 = (f32[512,256]{1,0:T(8,128)S(1)}, f32[512,256]{1,0:T(8,128)}, u32[]{:S(2)}) copy-start(f32[512,256]{1,0:T(8,128)} %copy-done.2) | copy-start | bytes 1572868
  86.7 1.0 copy-start.5
Sparse Core Ops, SparseCore 0:
  88.9 58.4 reduce-scatter.3
where the time goes:
time: 199 us
  waiting for transfers between devices  68.4 us (34%)
  blocking collectives  50.3 us (25%)
  starting transfers between devices  20.7 us (10%)
  matrix products  20.2 us (10%)
  between operations  14.5 us (7%)
  local copies, waits for them, and re-layouts  12.9 us (6%)
  other arithmetic  11.6 us (6%)
    unnamed x2, waiting for transfers between devices  46.8 us
    all_gather x1, blocking collectives, per_device(): lax.all_gather(weight_part, ('regroup', 'loop'), axis=0, tiled=True)  31.3 us
    ppermute x10, waiting for transfers between devices, shifted(): return lax.ppermute(block, axis, route)  18 us
    ppermute x10, starting transfers between devices, shifted(): return lax.ppermute(block, axis, route)  17.2 us
    psum x1, blocking collectives, per_device(): weight_part = lax.psum(weight_part, 'replica')  11.5 us
    dot_general x2, matrix products, from_nets(): jnp.einsum('tr,tif->rif', row_hot, per_tile, precision=high)  7.83 us
    dot_general x2, matrix products, to_nets(): return jnp.einsum('tc,tjf->cjf', hot, per_tile, precision=high)  7.66 us
    all_to_all x1, blocking collectives, per_device(): lax.all_to_all(grad_rows[None, None], 'regroup', split_axis=3, concat_axi...  7.56 us
  transfers between devices with their start and end apart: 12, of which 9 were waited for; matrix products, arithmetic and copies ran while one was open for 9% of the time, Pallas kernels for 0%

commit v1 on v0

--- a/solution.py
+++ b/solution.py
@@ -112,7 +112,7 @@
     weight_part = lax.psum_scatter(
         weight_term, ("regroup", "loop"), scatter_dimension=0, tiled=True
     )
-    weight_part = lax.psum(weight_part, "replica")
+    weight_part = jnp.sum(lax.all_gather(weight_part, "replica"), axis=0)
     weight_sum = lax.all_gather(weight_part, ("regroup", "loop"), axis=0, tiled=True)
     total_cells = cells * lax.axis_size("regroup") * loops * lax.axis_size("replica")
     grad_weight = weight_sum * (1.0 / math.sqrt(total_cells))

time: 199 us -> 192 us (0.965)
  blocking collectives: 50.3 us -> 44.5 us
    unnamed x2 -> x1, waiting for transfers between devices: 46.8 us -> 0.02 us
    reduce_scatter x0 -> x1, waiting for transfers between devices: none -> 46.7 us  [per_device(): lax.psum_scatter(weight_term, ('regroup', 'loop'), scatter_dimension=0, t...]
    psum x1 -> x0, blocking collectives: 11.5 us -> none  [per_device(): weight_part = lax.psum(weight_part, 'replica')]
    all_gather x0 -> x1, blocking collectives: none -> 5.62 us  [per_device(): weight_part = jnp.sum(lax.all_gather(weight_part, 'replica'), axis=0)]
    unnamed x51 -> x50, local copies, waits for them, and re-layouts: 7.11 us -> 6.26 us
  transfers between devices with their start and end apart: 12 -> 12, of which waited for: 9 -> 9; matrix products, arithmetic and copies ran while one was open for 9% -> 10% of each run, Pallas kernels for 0% -> 0%
where the time goes in v1:
time: 192 us
  waiting for transfers between devices  68.3 us (36%)
  blocking collectives  44.5 us (23%)
  starting transfers between devices  20.7 us (11%)
  matrix products  20.2 us (11%)
  between operations  14.5 us (8%)
  local copies, waits for them, and re-layouts  12 us (6%)
  other arithmetic  11.6 us (6%)
    reduce_scatter x1, waiting for transfers between devices, per_device(): lax.psum_scatter(weight_term, ('regroup', 'loop'), scatter_dimension=0, t...  46.7 us
    all_gather x1, blocking collectives, per_device(): lax.all_gather(weight_part, ('regroup', 'loop'), axis=0, tiled=True)  31.3 us
    ppermute x10, waiting for transfers between devices, shifted(): return lax.ppermute(block, axis, route)  18 us
    ppermute x10, starting transfers between devices, shifted(): return lax.ppermute(block, axis, route)  17.2 us
    dot_general x2, matrix products, from_nets(): jnp.einsum('tr,tif->rif', row_hot, per_tile, precision=high)  7.81 us
    dot_general x2, matrix products, to_nets(): return jnp.einsum('tc,tjf->cjf', hot, per_tile, precision=high)  7.66 us
    all_to_all x1, blocking collectives, per_device(): lax.all_to_all(grad_rows[None, None], 'regroup', split_axis=3, concat_axi...  7.56 us
    unnamed x50, local copies, waits for them, and re-layouts  6.26 us
  transfers between devices with their start and end apart: 12, of which 9 were waited for; matrix products, arithmetic and copies ran while one was open for 10% of the time, Pallas kernels for 0%

profile of v1, /device:TPU:0, one launch (start us, length us, event | category | flops | bytes accessed | tf_op | source)
XLA Modules:
  0.0 191.9 jit_solution(16814617880006446578)
XLA Ops:
  7.2 0.8 iota_compare_fusion
  8.0 0.7 compare_select_fusion.8
  8.6 1.6 convert_reduce_fusion
  10.3 0.1 convolution_convert_fusion.2
  10.4 0.6 slice_bitcast_fusion.4
  11.0 3.0 %collective-permute-start.2 = (bf16[128]{0:T(256)(128)(2,1)}, bf16[128]{0:T(256)(128)(2,1)}, u32[]{:S(2)}, u32[]{:S(2)}) collective-permute-start(bf16[128]{0:T(256)(128)(2,1)} %get-tuple-element.13), channel_id=1, source_target_pairs={{12,0},{0,4},{4,8},{8,12},{13,1},{1,5},{5,9},{9,13},{14,2},{2,6},{... | collective-permute-start | bytes 776 | tf_op jit(solution)/shard_map/ppermute | solution.py:13
  14.0 2.0 %collective-permute-start.3 = (bf16[128]{0:T(256)(128)(2,1)}, bf16[128]{0:T(256)(128)(2,1)}, u32[]{:S(2)}, u32[]{:S(2)}) collective-permute-start(bf16[128]{0:T(256)(128)(2,1)} %get-tuple-element.14), channel_id=1, source_target_pairs={{4,0},{8,4},{12,8},{0,12},{5,1},{9,5},{13,9},{1,13},{6,2},{10,6},{... | collective-permute-start | bytes 776 | tf_op jit(solution)/shard_map/ppermute | solution.py:13
  16.0 1.4 copy.129
  17.4 0.5 broadcast.232
  17.9 2.3 %reduce.1 = bf16[1024,128]{1,0:T(8,128)(2,1)S(1)} reduce(bf16[1024,1,1,128]{3,2,1,0:T(2,128)(2,1)S(1)} %bitcast.137, bf16[]{:T(256)} %broadcast.232), dimensions={1,2}, to_apply=%bitcast.132.reduce_sub_computation | reduce | bytes 524290
  20.2 0.8 reshape.233
  20.9 3.4 %all-to-all-start = ((bf16[2,2,32768]{2,1,0:T(2,128)(2,1)}), bf16[2,2,32768]{2,1,0:T(2,128)(2,1)S(1)}, u32[]{:S(2)}, u32[]{:S(2)}) async-start(bf16[2,2,32768]{2,1,0:T(2,128)(2,1)} %reshape.233), calls=%async_computation | async-start | bytes 524288 | tf_op jit(solution)/shard_map/all_to_all | solution.py:21
  24.4 0.6 fusion.43
  25.0 0.1 fusion.13
  25.2 0.8 copy.89
  25.9 3.6 %all-to-all-done = bf16[2,2,32768]{2,1,0:T(2,128)(2,1)S(1)} async-done(((bf16[2,2,32768]{2,1,0:T(2,128)(2,1)}), bf16[2,2,32768]{2,1,0:T(2,128)(2,1)S(1)}, u32[]{:S(2)}, u32[]{:S(2)}) %all-to-all-start) | async-done | bytes 262176 | tf_op jit(solution)/shard_map/all_to_all | solution.py:21
  29.5 0.3 reshape.234
  29.9 0.1 copy.84
  30.0 1.1 divide_convert_fusion
  31.1 0.7 gather_fusion
  31.8 0.5 copy-done.1
  32.3 0.8 fusion.23
  33.1 3.8 %fusion.9 = bf16[3,128,256]{2,0,1:T(4,128)(2,1)S(1)} fusion(f32[32,128,256]{2,1,0:T(8,128)S(1)} %fusion.23, s32[32]{0:T(128)S(1)} %copy-done.10), kind=kOutput, calls=%fused_computation.17 | convolution fusion | flops 37847136 | bytes 4391040 | tf_op jit(solution)/shard_map/tc,tjf->cjf/dot_general | solution.py:47
  37.0 0.3 fusion.54
  37.3 2.1 %collective-permute-start.1 = (bf16[128,256]{1,0:T(8,128)(2,1)S(1)}, bf16[128,256]{1,0:T(8,128)(2,1)S(1)}, u32[]{:S(2)}, u32[]{:S(2)}) collective-permute-start(bf16[128,256]{1,0:T(8,128)(2,1)S(1)} %bitcast.148), channel_id=1, source_target_pairs={{4,0},{8,4},{12,8},{0,12},{5,1},{9,5},{13,9},{1,13},{6,2},{10,6},{... | collective-permute-start | bytes 196616 | tf_op jit(solution)/shard_map/ppermute | solution.py:13
  39.4 0.7 fusion.48
  40.0 1.6 collective-permute-done.1
  41.6 3.8 %collective-permute-done = bf16[128,256]{1,0:T(8,128)(2,1)S(1)} collective-permute-done((bf16[128,256]{1,0:T(8,128)(2,1)S(1)}, bf16[128,256]{1,0:T(8,128)(2,1)S(1)}, u32[]{:S(2)}, u32[]{:S(2)}) %collective-permute-start) | collective-permute-done | bytes 65568 | tf_op jit(solution)/shard_map/ppermute | solution.py:13
  45.6 2.0 %collective-permute-start.4 = (bf16[128,256]{1,0:T(8,128)(2,1)S(1)}, bf16[128,256]{1,0:T(8,128)(2,1)S(1)}, u32[]{:S(2)}, u32[]{:S(2)}) collective-permute-start(bf16[128,256]{1,0:T(8,128)(2,1)S(1)} %fusion.27), channel_id=1, source_target_pairs={{12,0},{0,4},{4,8},{8,12},{13,1},{1,5},{5,9},{9,13},{14,2},{2,6},{... | collective-permute-start | bytes 196616 | tf_op jit(solution)/shard_map/ppermute | solution.py:13
  47.6 2.2 %collective-permute-done.5 = bf16[128,256]{1,0:T(8,128)(2,1)S(1)} collective-permute-done((bf16[128,256]{1,0:T(8,128)(2,1)S(1)}, bf16[128,256]{1,0:T(8,128)(2,1)S(1)}, u32[]{:S(2)}, u32[]{:S(2)}) %collective-permute-start.5) | collective-permute-done | bytes 65568 | tf_op jit(solution)/shard_map/ppermute | solution.py:13
  49.8 2.0 %collective-permute-done.4 = bf16[128,256]{1,0:T(8,128)(2,1)S(1)} collective-permute-done((bf16[128,256]{1,0:T(8,128)(2,1)S(1)}, bf16[128,256]{1,0:T(8,128)(2,1)S(1)}, u32[]{:S(2)}, u32[]{:S(2)}) %collective-permute-start.4) | collective-permute-done | bytes 65568 | tf_op jit(solution)/shard_map/ppermute | solution.py:13
  51.9 0.7 gather_fusion.1
  52.6 0.7 fusion.22
  53.5 4.0 %fusion.19 = (f32[4,128]{0,1:T(8,128)S(1)}, f32[4,128,256]{2,0,1:T(4,128)S(1)}) fusion(f32[4,128]{0,1:T(8,128)S(1)} %copy-done.8, f32[32,128,256]{2,1,0:T(8,128)S(1)} %fusion.22, s32[32]{0:T(128)S(1)} %bitcast.158), kind=kOutput, calls=%fused_computation.39 | convolution fusion | flops 50724480 | bytes 4722816 | tf_op jit(solution)/shard_map/tr,tif->rif/dot_general | solution.py:54
  57.5 0.1 copy.88
  57.7 1.1 multiply_reduce_fusion
  58.8 0.3 fusion.15
  59.1 0.5 copy-done.2
  59.6 0.7 gather_fusion.2
  60.3 0.8 fusion.21
  61.1 3.8 %fusion.2 = bf16[3,128,256]{2,0,1:T(4,128)(2,1)S(1)} fusion(f32[32,128,256]{2,1,0:T(8,128)S(1)} %fusion.21, s32[32]{0:T(128)S(1)} %copy-done.11), kind=kOutput, calls=%fused_computation.6 | convolution fusion | flops 37748832 | bytes 4391040 | tf_op jit(solution)/shard_map/tc,tjf->cjf/dot_general | solution.py:47
  65.0 3.8 %collective-permute-start.7 = (bf16[128,256]{1,0:T(8,128)(2,1)S(1)}, bf16[128,256]{1,0:T(8,128)(2,1)S(1)}, u32[]{:S(2)}, u32[]{:S(2)}) collective-permute-start(bf16[128,256]{1,0:T(8,128)(2,1)S(1)} %get-tuple-element.12), channel_id=1, source_target_pairs={{4,0},{8,4},{12,8},{0,12},{5,1},{9,5},{13,9},{1,13},{6,2},{10,6},{... | collective-permute-start | bytes 196616 | tf_op jit(solution)/shard_map/ppermute | solution.py:13
  68.8 2.2 %collective-permute-done.6 = bf16[128,256]{1,0:T(8,128)(2,1)S(1)} collective-permute-done((bf16[128,256]{1,0:T(8,128)(2,1)S(1)}, bf16[128,256]{1,0:T(8,128)(2,1)S(1)}, u32[]{:S(2)}, u32[]{:S(2)}) %collective-permute-start.6) | collective-permute-done | bytes 65568 | tf_op jit(solution)/shard_map/ppermute | solution.py:13
  71.2 4.2 %collective-permute-start.9 = (bf16[128,256]{1,0:T(8,128)(2,1)S(1)}, bf16[128,256]{1,0:T(8,128)(2,1)S(1)}, u32[]{:S(2)}, u32[]{:S(2)}) collective-permute-start(bf16[128,256]{1,0:T(8,128)(2,1)S(1)} %fusion.30), channel_id=1, source_target_pairs={{4,0},{8,4},{12,8},{0,12},{5,1},{9,5},{13,9},{1,13},{6,2},{10,6},{... | collective-permute-start | bytes 196616 | tf_op jit(solution)/shard_map/ppermute | solution.py:13
  75.3 1.9 collective-permute-done.9
  77.2 4.2 %collective-permute-done.8 = bf16[128,256]{1,0:T(8,128)(2,1)S(1)} collective-permute-done((bf16[128,256]{1,0:T(8,128)(2,1)S(1)}, bf16[128,256]{1,0:T(8,128)(2,1)S(1)}, u32[]{:S(2)}, u32[]{:S(2)}) %collective-permute-start.8) | collective-permute-done | bytes 65568 | tf_op jit(solution)/shard_map/ppermute | solution.py:13
  81.4 0.7 gather_fusion.3
  82.1 0.7 fusion.20
  82.9 3.8 %fusion = f32[4,128,256]{2,0,1:T(4,128)S(1)} fusion(f32[32,128,256]{2,1,0:T(8,128)S(1)} %fusion.20, s32[32]{0:T(128)S(1)} %bitcast.159), kind=kOutput, calls=%fused_computation.4 | convolution fusion | flops 50331776 | bytes 4718720 | tf_op jit(solution)/shard_map/tr,tif->rif/dot_general | solution.py:54
  86.8 0.1 fusion.18
  87.0 0.7 copy-done.5
  87.6 0.3 convolution_bitcast_fusion
  87.9 0.8 copy.101
  88.8 0.3 fusion.12
  89.0 0.5 copy.96
  89.5 2.3 %reduce.2 = bf16[256,512]{1,0:T(8,128)(2,1)S(1)} reduce(bf16[256,1,1,512]{3,2,1,0:T(2,128)(2,1)S(1)} %bitcast.138, bf16[]{:T(256)} %broadcast.232), dimensions={1,2}, to_apply=%bitcast.111.reduce_sub_computation | reduce | bytes 524290
  91.8 0.2 reshape.235
  91.9 7.6 %all_to_all.33 = bf16[2,2,32768]{2,1,0:T(2,128)(2,1)S(1)} all-to-all(bf16[2,2,32768]{2,1,0:T(2,128)(2,1)S(1)} %reshape.235), channel_id=1, replica_groups=mesh['regroup'=2,'loop'=4,'replica'=4] {'regroup'}, dimensions={0} | all-to-all | bytes 524288 | tf_op jit(solution)/shard_map/all_to_all | solution.py:108
  99.5 0.3 reshape.236
  99.8 0.8 copy.97
  100.7 46.7 %reduce-scatter.4.cloned.1.call-done = f32[32,256]{1,0:T(8,128)} async-done(((f32[256,256]{1,0:T(8,128)}), f32[32,256]{1,0:T(8,128)}) %reduce-scatter.4.cloned.1.call-update) | async-done | bytes 32784 | tf_op jit(solution)/shard_map/reduce_scatter | solution.py:112
  147.4 5.6 %all-gather = f32[128,256]{1,0:T(8,128)S(1)} all-gather(f32[32,256]{1,0:T(8,128)} %reduce-scatter.4.cloned.1.call-done), channel_id=2, replica_groups=mesh['regroup'=2,'loop'=4,'replica'=4] {'replica'}, dimensions={0}, use_global_device_ids=true | all-gather | bytes 163840 | tf_op jit(solution)/shard_map/all_gather | solution.py:115
  153.0 31.3 %all_gather.11 = f32[256,256]{1,0:T(8,128)S(1)} all-gather(f32[32,256]{1,0:T(8,128)S(1)} %reduce_sum.53), channel_id=1, replica_groups=mesh['regroup'=2,'loop'=4,'replica'=4] {'regroup','loop'}, dimensions={0}, use_global_device_ids=true | all-gather | bytes 294912 | tf_op jit(solution)/shard_map/all_gather | solution.py:116
  184.3 0.7 broadcast_multiply_fusion
  (63 shorter events, 1.0 us)
Async XLA Ops:
  7.2 22.9 %copy-start = (bf16[256,256]{1,0:T(8,128)(2,1)S(1)}, bf16[256,256]{1,0:T(8,128)(2,1)}, u32[]{:S(2)}) copy-start(bf16[256,256]{1,0:T(8,128)(2,1)} %param.8) | copy-start | bytes 393220
  7.2 17.3 %copy-start.18 = (s32[1,1,1,32]{3,2,1,0:T(1,128)S(1)}, s32[1,1,1,32]{3,2,1,0:T(1,128)}, u32[]{:S(2)}) copy-start(s32[1,1,1,32]{3,2,1,0:T(1,128)} %param.11) | copy-start | bytes 388
  7.2 17.8 %copy-start.14 = (s32[1,1,1,32]{3,2,1,0:T(1,128)S(1)}, s32[1,1,1,32]{3,2,1,0:T(1,128)}, u32[]{:S(2)}) copy-start(s32[1,1,1,32]{3,2,1,0:T(1,128)} %param.10) | copy-start | bytes 388
  8.6 16.4 %copy-start.9 = (s32[32]{0:T(128)}, s32[32]{0:T(128)S(1)}, u32[]{:S(2)}) copy-start(s32[32]{0:T(128)S(1)} %compare_select_fusion.8) | copy-start | bytes 388
  11.0 28.4 %collective-permute-start.2 = (bf16[128]{0:T(256)(128)(2,1)}, bf16[128]{0:T(256)(128)(2,1)}, u32[]{:S(2)}, u32[]{:S(2)}) collective-permute-start(bf16[128]{0:T(256)(128)(2,1)} %get-tuple-element.13), channel_id=1, source_target_pairs={{12,0},{0,4},{4,8},{8,12},{13,1},{1,5},{5,9},{9,13},{14,2},{2,6},{... | collective-permute-start | bytes 776 | tf_op jit(solution)/shard_map/ppermute | solution.py:13
  14.0 25.4 %collective-permute-start.3 = (bf16[128]{0:T(256)(128)(2,1)}, bf16[128]{0:T(256)(128)(2,1)}, u32[]{:S(2)}, u32[]{:S(2)}) collective-permute-start(bf16[128]{0:T(256)(128)(2,1)} %get-tuple-element.14), channel_id=1, source_target_pairs={{4,0},{8,4},{12,8},{0,12},{5,1},{9,5},{13,9},{1,13},{6,2},{10,6},{... | collective-permute-start | bytes 776 | tf_op jit(solution)/shard_map/ppermute | solution.py:13
  20.9 8.6 %all-to-all-start = ((bf16[2,2,32768]{2,1,0:T(2,128)(2,1)}), bf16[2,2,32768]{2,1,0:T(2,128)(2,1)S(1)}, u32[]{:S(2)}, u32[]{:S(2)}) async-start(bf16[2,2,32768]{2,1,0:T(2,128)(2,1)} %reshape.233), calls=%async_computation | async-start | bytes 524288 | tf_op jit(solution)/shard_map/all_to_all | solution.py:21
  24.4 123.0 %reduce-scatter.4.cloned.1.call-start = ((), (), s32[]{:S(2)}) async-start(), calls=%async_computation.3 | async-start | bytes 294912 | tf_op jit(solution)/shard_map/reduce_scatter | solution.py:112
  30.0 1.1 copy-start.4
  31.1 1.2 copy-start.1
  32.3 0.8 copy-start.10
  33.1 14.5 %copy-start.17 = (s32[32]{0:T(128)S(1)}, s32[32]{0:T(128)}, u32[]{:S(2)}) copy-start(s32[32]{0:T(128)} %fusion.43) | copy-start | bytes 388
  37.3 4.3 %collective-permute-start.1 = (bf16[128,256]{1,0:T(8,128)(2,1)S(1)}, bf16[128,256]{1,0:T(8,128)(2,1)S(1)}, u32[]{:S(2)}, u32[]{:S(2)}) collective-permute-start(bf16[128,256]{1,0:T(8,128)(2,1)S(1)} %bitcast.148), channel_id=1, source_target_pairs={{4,0},{8,4},{12,8},{0,12},{5,1},{9,5},{13,9},{1,13},{6,2},{10,6},{... | collective-permute-start | bytes 196616 | tf_op jit(solution)/shard_map/ppermute | solution.py:13
  39.4 6.1 %collective-permute-start = (bf16[128,256]{1,0:T(8,128)(2,1)S(1)}, bf16[128,256]{1,0:T(8,128)(2,1)S(1)}, u32[]{:S(2)}, u32[]{:S(2)}) collective-permute-start(bf16[128,256]{1,0:T(8,128)(2,1)S(1)} %bitcast.147), channel_id=1, source_target_pairs={{12,0},{0,4},{4,8},{8,12},{13,1},{1,5},{5,9},{9,13},{14,2},{2,6},{... | collective-permute-start | bytes 196616 | tf_op jit(solution)/shard_map/ppermute | solution.py:13
  40.0 11.9 %copy-start.12 = (f32[128]{0:T(128)}, f32[128]{0:T(128)S(1)}, u32[]{:S(2)}) copy-start(f32[128]{0:T(128)S(1)} %fusion.48) | copy-start | bytes 1540
  45.5 4.3 %collective-permute-start.5 = (bf16[128,256]{1,0:T(8,128)(2,1)S(1)}, bf16[128,256]{1,0:T(8,128)(2,1)S(1)}, u32[]{:S(2)}, u32[]{:S(2)}) collective-permute-start(bf16[128,256]{1,0:T(8,128)(2,1)S(1)} %fusion.27), channel_id=1, source_target_pairs={{4,0},{8,4},{12,8},{0,12},{5,1},{9,5},{13,9},{1,13},{6,2},{10,6},{... | collective-permute-start | bytes 196616 | tf_op jit(solution)/shard_map/ppermute | solution.py:13
  45.6 6.3 %collective-permute-start.4 = (bf16[128,256]{1,0:T(8,128)(2,1)S(1)}, bf16[128,256]{1,0:T(8,128)(2,1)S(1)}, u32[]{:S(2)}, u32[]{:S(2)}) collective-permute-start(bf16[128,256]{1,0:T(8,128)(2,1)S(1)} %fusion.27), channel_id=1, source_target_pairs={{12,0},{0,4},{4,8},{8,12},{13,1},{1,5},{5,9},{9,13},{14,2},{2,6},{... | collective-permute-start | bytes 196616 | tf_op jit(solution)/shard_map/ppermute | solution.py:13
  52.6 0.8 copy-start.8
  52.6 0.8 copy-start.15
  53.5 4.2 %copy-start.6 = (f32[512,256]{1,0:T(8,128)S(1)}, f32[512,256]{1,0:T(8,128)}, u32[]{:S(2)}) copy-start(f32[512,256]{1,0:T(8,128)} %get-tuple-element.16) | copy-start | bytes 1572868
  53.5 4.2 %copy-start.7 = (bf16[1,1,1,512,256]{4,3,2,1,0:T(8,128)(2,1)S(1)}, bf16[1,1,1,512,256]{4,3,2,1,0:T(8,128)(2,1)}, u32[]{:S(2)}) copy-start(bf16[1,1,1,512,256]{4,3,2,1,0:T(8,128)(2,1)} %param.13) | copy-start | bytes 786436
  58.8 0.8 copy-start.2
  60.3 0.8 copy-start.11
  61.1 10.0 %copy-start.13 = (f32[128]{0:T(128)S(1)}, f32[128]{0:T(128)}, u32[]{:S(2)}) copy-start(f32[128]{0:T(128)} %copy-done.12) | copy-start | bytes 1540
  65.0 6.1 %collective-permute-start.6 = (bf16[128,256]{1,0:T(8,128)(2,1)S(1)}, bf16[128,256]{1,0:T(8,128)(2,1)S(1)}, u32[]{:S(2)}, u32[]{:S(2)}) collective-permute-start(bf16[128,256]{1,0:T(8,128)(2,1)S(1)} %get-tuple-element.11), channel_id=1, source_target_pairs={{12,0},{0,4},{4,8},{8,12},{13,1},{1,5},{5,9},{9,13},{14,2},{2,6},{... | collective-permute-start | bytes 196616 | tf_op jit(solution)/shard_map/ppermute | solution.py:13
  65.0 6.1 %collective-permute-start.7 = (bf16[128,256]{1,0:T(8,128)(2,1)S(1)}, bf16[128,256]{1,0:T(8,128)(2,1)S(1)}, u32[]{:S(2)}, u32[]{:S(2)}) collective-permute-start(bf16[128,256]{1,0:T(8,128)(2,1)S(1)} %get-tuple-element.12), channel_id=1, source_target_pairs={{4,0},{8,4},{12,8},{0,12},{5,1},{9,5},{13,9},{1,13},{6,2},{10,6},{... | collective-permute-start | bytes 196616 | tf_op jit(solution)/shard_map/ppermute | solution.py:13
  71.2 6.1 %collective-permute-start.9 = (bf16[128,256]{1,0:T(8,128)(2,1)S(1)}, bf16[128,256]{1,0:T(8,128)(2,1)S(1)}, u32[]{:S(2)}, u32[]{:S(2)}) collective-permute-start(bf16[128,256]{1,0:T(8,128)(2,1)S(1)} %fusion.30), channel_id=1, source_target_pairs={{4,0},{8,4},{12,8},{0,12},{5,1},{9,5},{13,9},{1,13},{6,2},{10,6},{... | collective-permute-start | bytes 196616 | tf_op jit(solution)/shard_map/ppermute | solution.py:13
  75.3 6.1 %collective-permute-start.8 = (bf16[128,256]{1,0:T(8,128)(2,1)S(1)}, bf16[128,256]{1,0:T(8,128)(2,1)S(1)}, u32[]{:S(2)}, u32[]{:S(2)}) collective-permute-start(bf16[128,256]{1,0:T(8,128)(2,1)S(1)} %fusion.30), channel_id=1, source_target_pairs={{12,0},{0,4},{4,8},{8,12},{13,1},{1,5},{5,9},{9,13},{14,2},{2,6},{... | collective-permute-start | bytes 196616 | tf_op jit(solution)/shard_map/ppermute | solution.py:13
  82.1 0.7 copy-start.16
  82.8 3.9 %copy-start.3 = (f32[512,256]{1,0:T(8,128)S(1)}, f32[512,256]{1,0:T(8,128)}, u32[]{:S(2)}) copy-start(f32[512,256]{1,0:T(8,128)} %copy-done.2) | copy-start | bytes 1572868
  86.7 1.0 copy-start.5
Sparse Core Ops, SparseCore 0:
  88.9 58.4 reduce-scatter.3
